TPU v7x, 32 devices: a whole 2x2x4 slice. The times are simulated.
32 devices in a mesh: row: 4 (over y, x), col: 8 (over z, core).
Axes of the slice: x: 2, y: 2, z: 4, core: 2. Of those that a mesh axis runs over, the one named last changes fastest.
Arguments:
- slab: bfloat16 [1024, 16384], P(('row', 'col')), may hold values from -0.1875 to 0.1875
- block_mask: int32 [32, 16], P(('row', 'col')), may hold values 0 or 1
- damping: float32 [16384], replicated, may hold values from 0.05 to 2
Outputs:
- hessian: float32 [16384, 16384], P('row', 'col')
All inputs are finite; a program needn't handle non-finite values. No bound on the sum of `block_mask` on one device may be relied on, other than what follows from the above.
Results may differ from a plain program's by a relative error of at most 0.0003.
Values may be sent and summed in bfloat16 or wider, within the bound.
No kernel may reach another device: no remote copies, remote signals or barrier semaphores. Data moves between devices by JAX's collectives and lax.ppermute only.
A program may use at most 128 MiB of HBM per device.

v0:
```python
import jax
import jax.numpy as jnp
from jax import lax
from jax.sharding import PartitionSpec as P


def shards(slab, block_mask, damping):
    local_rows = slab.shape[0]
    width = slab.shape[1]
    row_count = lax.axis_size("row")
    col_count = lax.axis_size("col")
    row_width = width // row_count
    col_width = width // col_count
    block_count = block_mask.shape[1]
    column_mask = jnp.repeat(block_mask[0], width // block_count).astype(jnp.bfloat16)
    masked = slab * column_mask[None, :]
    row_parts = masked.reshape(local_rows, row_count, row_width)
    row_parts = lax.all_to_all(row_parts, "row", split_axis=1, concat_axis=0, tiled=True)
    row_parts = row_parts.reshape(row_count * local_rows, row_width)
    row_panel = lax.all_gather(row_parts, "col", axis=0, tiled=True)
    row_panel = row_panel.reshape(col_count, row_count, local_rows, row_width)
    row_panel = jnp.transpose(row_panel, (1, 0, 2, 3)).reshape(
        row_count * col_count * local_rows, row_width
    )
    col_parts = masked.reshape(local_rows, col_count, col_width)
    col_parts = lax.all_to_all(col_parts, "col", split_axis=1, concat_axis=0, tiled=True)
    col_parts = col_parts.reshape(col_count * local_rows, col_width)
    block = lax.dot_general(
        row_panel,
        lax.all_gather(col_parts, "row", axis=0, tiled=True),
        (((0,), (0,)), ((), ())),
        preferred_element_type=jnp.float32,
    )
    row_start = lax.axis_index("row") * row_width
    col_start = lax.axis_index("col") * col_width
    global_rows = row_start + jnp.arange(row_width, dtype=jnp.int32)
    global_cols = col_start + jnp.arange(col_width, dtype=jnp.int32)
    row_damping = lax.dynamic_slice_in_dim(damping, row_start, row_width, 0)
    on_diagonal = global_rows[:, None] == global_cols[None, :]
    return block + jnp.where(on_diagonal, row_damping[:, None], jnp.float32(0.0))


def solution(mesh):
    placed = (P(("row", "col"), None), P(("row", "col"), None), P())
    return jax.shard_map(
        shards, mesh=mesh, in_specs=placed, out_specs=P("row", "col"), check_vma=False
    )
```

profile of v0, /device:TPU:0, one launch (start us, length us, event | category | flops | bytes accessed | tf_op | source)
XLA Modules:
  0.0 214.2 jit_solution(16617587774653621209)
XLA Ops:
  6.5 0.0 all-gather.3.cloned.1.call-start
  6.5 0.7 convert_bitcast_fusion
  7.2 0.1 broadcast_bitcast_fusion
  7.3 1.4 broadcast_multiply_fusion
  8.6 0.1 copy.17
  8.7 19.2 %all_to_all.30 = bf16[32,4,4096]{2,0,1:T(8,128)(2,1)} all-to-all(bf16[32,4,4096]{2,0,1:T(8,128)(2,1)S(1)} %bitcast.36), channel_id=1, replica_groups=mesh['row'=4,'col'=8] {'row'}, dimensions={1} | all-to-all | bytes 2097152 | tf_op jit(solution)/shard_map/all_to_all | solution.py:18
  27.9 0.0 all-gather.3.cloned.1.call-update
  28.0 0.0 all-gather.5.cloned.1.call-start
  28.0 0.1 copy.16
  28.1 54.8 %all_to_all.31 = bf16[32,8,2048]{2,0,1:T(8,128)(2,1)} all-to-all(bf16[32,8,2048]{2,0,1:T(8,128)(2,1)S(1)} %bitcast.35), channel_id=1, replica_groups=mesh['row'=4,'col'=8] {'col'}, dimensions={1} | all-to-all | bytes 2097152 | tf_op jit(solution)/shard_map/all_to_all | solution.py:26
  82.9 0.0 all-gather.5.cloned.1.call-update
  82.9 45.7 %all-gather.3.cloned.1.call-done = bf16[1024,4096]{1,0:T(8,128)(2,1)} async-done(((bf16[128,4096]{1,0:T(8,128)(2,1)}), bf16[1024,4096]{1,0:T(8,128)(2,1)}) %all-gather.3.cloned.1.call-update) | async-done | bytes 8388624 | tf_op jit(solution)/shard_map/all_gather | solution.py:20
  128.7 0.0 dynamic-slice-start
  128.7 8.2 %copy.9 = bf16[8,4,32,4096]{3,2,0,1:T(8,128)(2,1)} copy(bf16[8,4,32,4096]{3,2,1,0:T(8,128)(2,1)} %bitcast.31) | data formatting | bytes 16777216 | tf_op jit(solution)/shard_map/reshape | solution.py:21
  136.9 43.8 %all-gather.5.cloned.1.call-done = bf16[1024,2048]{1,0:T(8,128)(2,1)} async-done(((bf16[256,2048]{1,0:T(8,128)(2,1)}), bf16[1024,2048]{1,0:T(8,128)(2,1)}) %all-gather.5.cloned.1.call-update) | async-done | bytes 4194320 | tf_op jit(solution)/shard_map/all_gather | solution.py:30
  180.7 0.0 dynamic-slice-done
  180.7 26.7 %select_add_fusion = f32[4096,2048]{1,0:T(8,128)} fusion(bf16[1024,4096]{1,0:T(8,128)(2,1)} %bitcast.32, bf16[1024,2048]{1,0:T(8,128)(2,1)} %all-gather.5.cloned.1.call-done, f32[4096]{0:T(1024)S(1)} %dynamic-slice-done, s32[2048]{0:T(1024)S(1)} %iota_add_fusion.1, s32[4096]{0:T(1024)S(1)} %iota_add_fusion), kind=kOutput, calls=%fused_computation | convolution fusion | flops 17205035008 | bytes 46178304 | tf_op jit(solution)/shard_map/dot_general | solution.py:28
  (3 shorter events, 0.0 us)
Async XLA Ops:
  6.5 122.1 %all-gather.3.cloned.1.call-start = ((), (), s32[]{:S(2)}) async-start(), calls=%async_computation.2 | async-start | bytes 9437184 | tf_op jit(solution)/shard_map/all_gather | solution.py:20
  28.0 152.7 %all-gather.5.cloned.1.call-start = ((), (), s32[]{:S(2)}) async-start(), calls=%async_computation.3 | async-start | bytes 5242880 | tf_op jit(solution)/shard_map/all_gather | solution.py:30
  128.7 52.0 %dynamic-slice-start = ((f32[16384]{0:T(1024)}, s32[]{:T(128)}), f32[4096]{0:T(1024)S(1)}, s32[]{:S(2)}) async-start(f32[16384]{0:T(1024)} %param.5, s32[]{:T(128)} %select_n.7), calls=%async_computation.4 | async-start | bytes 33280 | tf_op jit(solution)/shard_map/dynamic_slice | solution.py:38
Sparse Core Ops, SparseCore 0:
  28.1 100.5 all-gather.2
  130.5 50.1 all-gather.4
where the time goes:
time: 214 us
  waiting for transfers between devices  89.5 us (42%)
  blocking collectives  74 us (35%)
  matrix products  26.7 us (12%)
  between operations  13.4 us (6%)
  local copies, waits for them, and re-layouts  8.49 us (4%)
    all_to_all x1, blocking collectives, shards(): lax.all_to_all(col_parts, 'col', split_axis=1, concat_axis=0, tiled=True)  54.8 us
    all_gather x1, waiting for transfers between devices, shards(): row_panel = lax.all_gather(row_parts, 'col', axis=0, tiled=True)  45.7 us
    all_gather x1, waiting for transfers between devices, shards(): lax.all_gather(col_parts, 'row', axis=0, tiled=True)  43.8 us
    dot_general x1, matrix products, shards(): lax.dot_general(row_panel, lax.all_gather(col_parts, 'row', axis=0, tiled...  26.7 us
    all_to_all x1, blocking collectives, shards(): lax.all_to_all(row_parts, 'row', split_axis=1, concat_axis=0, tiled=True)  19.2 us
    reshape x1, local copies, waits for them, and re-layouts, shards(): row_panel = row_panel.reshape(col_count, row_count, local_rows, row_width)  8.21 us
  transfers between devices with their start and end apart: 2, of which 2 were waited for; matrix products, arithmetic and copies ran while one was open for 4% of the time, Pallas kernels for 0%

commit v1 on v0

--- a/solution.py
+++ b/solution.py
@@ -23,7 +23,19 @@
         row_count * col_count * local_rows, row_width
     )
     col_parts = masked.reshape(local_rows, col_count, col_width)
-    col_parts = lax.all_to_all(col_parts, "col", split_axis=1, concat_axis=0, tiled=True)
+    ways, here = (lax.axis_size("col"), lax.axis_index("col"))
+    width_2 = col_parts.shape[1] // ways
+    shape = list(col_parts.shape)
+    shape[1] = width_2
+    height = shape[0]
+    shape[0] = height * ways
+    full = jnp.zeros(shape, col_parts.dtype)
+    for mask in range(ways):
+        part = lax.dynamic_slice_in_dim(col_parts, (here ^ mask) * width_2, width_2, axis=1)
+        if mask:
+            part = lax.ppermute(part, "col", [(d, d ^ mask) for d in range(ways)])
+        full = lax.dynamic_update_slice_in_dim(full, part, (here ^ mask) * height, axis=0)
+    col_parts = full
     col_parts = col_parts.reshape(col_count * local_rows, col_width)
     block = lax.dot_general(
         row_panel,

time: 214 us -> 236 us (1.10)
  waiting for transfers between devices: 89.5 us -> 145 us
  blocking collectives: 74 us -> 19.2 us
  starting transfers between devices: 0.04 us -> 14.6 us
  local copies, waits for them, and re-layouts: 8.49 us -> 14.7 us
    ppermute x0 -> x7, waiting for transfers between devices: none -> 88.4 us  [shards(): part = lax.ppermute(part, 'col', [(d, d ^ mask) for d in range(ways)])]
    all_to_all x1 -> x0, blocking collectives: 54.8 us -> none  [shards(): lax.all_to_all(col_parts, 'col', split_axis=1, concat_axis=0, tiled=True)]
    all_gather x1, waiting for transfers between devices: 45.7 us -> 12.4 us  [shards(): row_panel = lax.all_gather(row_parts, 'col', axis=0, tiled=True)]
    ppermute x0 -> x7, starting transfers between devices: none -> 14.6 us  [shards(): part = lax.ppermute(part, 'col', [(d, d ^ mask) for d in range(ways)])]
    dynamic_slice x0 -> x1, local copies, waits for them, and re-layouts: none -> 3.13 us  [shards(): lax.dynamic_slice_in_dim(col_parts, (here ^ mask) * width_2, width_2, axi...]
  transfers between devices with their start and end apart: 2 -> 9, of which waited for: 2 -> 6; matrix products, arithmetic and copies ran while one was open for 4% -> 6% of each run, Pallas kernels for 0% -> 0%
where the time goes in v1:
time: 236 us
  waiting for transfers between devices  145 us (61%)
  matrix products  26.7 us (11%)
  blocking collectives  19.2 us (8%)
  local copies, waits for them, and re-layouts  14.7 us (6%)
  starting transfers between devices  14.6 us (6%)
  between operations  13.7 us (6%)
    ppermute x7, waiting for transfers between devices, shards(): part = lax.ppermute(part, 'col', [(d, d ^ mask) for d in range(ways)])  88.4 us
    all_gather x1, waiting for transfers between devices, shards(): lax.all_gather(col_parts, 'row', axis=0, tiled=True)  44.1 us
    dot_general x1, matrix products, shards(): lax.dot_general(row_panel, lax.all_gather(col_parts, 'row', axis=0, tiled...  26.7 us
    all_to_all x1, blocking collectives, shards(): lax.all_to_all(row_parts, 'row', split_axis=1, concat_axis=0, tiled=True)  19.2 us
    ppermute x7, starting transfers between devices, shards(): part = lax.ppermute(part, 'col', [(d, d ^ mask) for d in range(ways)])  14.6 us
    all_gather x1, waiting for transfers between devices, shards(): row_panel = lax.all_gather(row_parts, 'col', axis=0, tiled=True)  12.4 us
    reshape x1, local copies, waits for them, and re-layouts, shards(): row_panel = row_panel.reshape(col_count, row_count, local_rows, row_width)  8.09 us
  transfers between devices with their start and end apart: 9, of which 6 were waited for; matrix products, arithmetic and copies ran while one was open for 6% of the time, Pallas kernels for 0%

profile of v1, /device:TPU:0, one launch (start us, length us, event | category | flops | bytes accessed | tf_op | source)
XLA Modules:
  0.0 235.8 jit_solution(3824276108405293901)
XLA Ops:
  6.5 0.0 all-gather.3.cloned.1.call-start
  6.5 0.7 convert_bitcast_fusion
  7.2 0.1 broadcast_bitcast_fusion
  7.3 1.4 broadcast_multiply_fusion
  8.6 0.1 copy.29
  8.7 19.2 %all_to_all.15 = bf16[32,4,4096]{2,0,1:T(8,128)(2,1)} all-to-all(bf16[32,4,4096]{2,0,1:T(8,128)(2,1)S(1)} %bitcast.44), channel_id=1, replica_groups=mesh['row'=4,'col'=8] {'row'}, dimensions={1} | all-to-all | bytes 2097152 | tf_op jit(solution)/shard_map/all_to_all | solution.py:18
  27.9 0.0 all-gather.3.cloned.1.call-update
  28.0 0.0 all-gather.5.cloned.1.call-start
  28.1 0.6 copy.19
  28.7 3.1 %constant_dynamic-slice_fusion = (bf16[32,1,2048]{2,1,0:T(2,128)(2,1)S(1)}, bf16[32,1,2048]{2,1,0:T(2,128)(2,1)S(1)}, bf16[32,1,2048]{2,1,0:T(2,128)(2,1)S(1)}, ...) fusion(bf16[32,8,2048]{2,1,0:T(8,128)(2,1)S(1)} %bitcast.38, ...), kind=kLoop, calls=%fused_computation.14 | loop fusion | bytes 2097184 | tf_op jit(solution)/shard_map/dynamic_slice | solution.py:34
  31.8 1.5 collective-permute-start.6
  33.3 2.1 collective-permute-start.5
  35.5 0.4 collective-permute-start.4
  35.9 2.2 collective-permute-start.3
  38.1 0.2 collective-permute-start
  38.2 0.1 reshape.72
  38.3 0.1 bitcast_dynamic-update-slice_fusion.7
  38.5 1.4 collective-permute-done
  39.9 1.3 collective-permute-start.1
  41.3 1.0 bitcast_dynamic-update-slice_fusion.6
  42.3 43.1 %collective-permute-done.1 = bf16[32,1,2048]{2,1,0:T(2,128)(2,1)S(1)} collective-permute-done((bf16[32,1,2048]{2,1,0:T(2,128)(2,1)}, bf16[32,1,2048]{2,1,0:T(2,128)(2,1)S(1)}, u32[]{:S(2)}, u32[]{:S(2)}) %collective-permute-start.1) | collective-permute-done | bytes 131104 | tf_op jit(solution)/shard_map/ppermute | solution.py:36
  85.4 6.8 %collective-permute-start.2 = (bf16[32,1,2048]{2,1,0:T(2,128)(2,1)}, bf16[32,1,2048]{2,1,0:T(2,128)(2,1)S(1)}, u32[]{:S(2)}, u32[]{:S(2)}) collective-permute-start(bf16[32,1,2048]{2,1,0:T(2,128)(2,1)} %get-tuple-element.9), channel_id=1, source_target_pairs={{0,3},{1,2},{2,1},{3,0},{4,7},{5,6},{6,5},{7,4},{8,11},{9,10},{10,... | collective-permute-start | bytes 393224 | tf_op jit(solution)/shard_map/ppermute | solution.py:36
  92.3 0.1 bitcast_dynamic-update-slice_fusion.5
  92.3 25.6 %collective-permute-done.2 = bf16[32,1,2048]{2,1,0:T(2,128)(2,1)S(1)} collective-permute-done((bf16[32,1,2048]{2,1,0:T(2,128)(2,1)}, bf16[32,1,2048]{2,1,0:T(2,128)(2,1)S(1)}, u32[]{:S(2)}, u32[]{:S(2)}) %collective-permute-start.2) | collective-permute-done | bytes 131104 | tf_op jit(solution)/shard_map/ppermute | solution.py:36
  118.0 0.1 bitcast_dynamic-update-slice_fusion.4
  118.1 18.1 %collective-permute-done.3 = bf16[32,1,2048]{2,1,0:T(2,128)(2,1)S(1)} collective-permute-done((bf16[32,1,2048]{2,1,0:T(2,128)(2,1)S(1)}, bf16[32,1,2048]{2,1,0:T(2,128)(2,1)S(1)}, u32[]{:S(2)}, u32[]{:S(2)}) %collective-permute-start.3) | collective-permute-done | bytes 131104 | tf_op jit(solution)/shard_map/ppermute | solution.py:36
  136.2 0.1 bitcast_dynamic-update-slice_fusion.3
  136.3 0.0 collective-permute-done.4
  136.3 0.1 bitcast_dynamic-update-slice_fusion.2
  136.4 0.0 collective-permute-done.5
  136.4 0.1 bitcast_dynamic-update-slice_fusion.1
  136.5 0.0 collective-permute-done.6
  136.5 0.1 bitcast_dynamic-update-slice_fusion
  136.6 0.0 copy-start
  136.6 1.0 copy-done
  137.6 0.0 all-gather.5.cloned.1.call-update
  137.6 12.4 %all-gather.3.cloned.1.call-done = bf16[1024,4096]{1,0:T(8,128)(2,1)} async-done(((bf16[128,4096]{1,0:T(8,128)(2,1)}), bf16[1024,4096]{1,0:T(8,128)(2,1)}) %all-gather.3.cloned.1.call-update) | async-done | bytes 8388624 | tf_op jit(solution)/shard_map/all_gather | solution.py:20
  150.0 0.0 dynamic-slice-start
  150.0 8.1 %copy.8 = bf16[8,4,32,4096]{3,2,0,1:T(8,128)(2,1)} copy(bf16[8,4,32,4096]{3,2,1,0:T(8,128)(2,1)} %bitcast.41) | data formatting | bytes 16777216 | tf_op jit(solution)/shard_map/reshape | solution.py:21
  158.1 44.1 %all-gather.5.cloned.1.call-done = bf16[1024,2048]{1,0:T(8,128)(2,1)} async-done(((bf16[256,2048]{1,0:T(8,128)(2,1)}), bf16[1024,2048]{1,0:T(8,128)(2,1)}) %all-gather.5.cloned.1.call-update) | async-done | bytes 4194320 | tf_op jit(solution)/shard_map/all_gather | solution.py:42
  202.2 0.0 dynamic-slice-done
  202.2 26.7 %select_add_fusion = f32[4096,2048]{1,0:T(8,128)} fusion(bf16[1024,4096]{1,0:T(8,128)(2,1)} %bitcast.42, bf16[1024,2048]{1,0:T(8,128)(2,1)} %all-gather.5.cloned.1.call-done, f32[4096]{0:T(1024)S(1)} %dynamic-slice-done, s32[2048]{0:T(1024)S(1)} %iota_add_fusion.1, s32[4096]{0:T(1024)S(1)} %iota_add_fusion), kind=kOutput, calls=%fused_computation | convolution fusion | flops 17205035008 | bytes 46178304 | tf_op jit(solution)/shard_map/dot_general | solution.py:40
  (3 shorter events, 0.0 us)
Async XLA Ops:
  6.5 143.5 %all-gather.3.cloned.1.call-start = ((), (), s32[]{:S(2)}) async-start(), calls=%async_computation.1 | async-start | bytes 9437184 | tf_op jit(solution)/shard_map/all_gather | solution.py:20
  28.0 174.2 %all-gather.5.cloned.1.call-start = ((), (), s32[]{:S(2)}) async-start(), calls=%async_computation.2 | async-start | bytes 5242880 | tf_op jit(solution)/shard_map/all_gather | solution.py:42
  31.8 104.7 %collective-permute-start.6 = (bf16[32,1,2048]{2,1,0:T(2,128)(2,1)S(1)}, bf16[32,1,2048]{2,1,0:T(2,128)(2,1)S(1)}, u32[]{:S(2)}, u32[]{:S(2)}) collective-permute-start(bf16[32,1,2048]{2,1,0:T(2,128)(2,1)S(1)} %get-tuple-element.5), channel_id=1, source_target_pairs={{0,7},{1,6},{2,5},{3,4},{4,3},{5,2},{6,1},{7,0},{8,15},{9,14},{10,... | collective-permute-start | bytes 393224 | tf_op jit(solution)/shard_map/ppermute | solution.py:36
  33.3 103.1 %collective-permute-start.5 = (bf16[32,1,2048]{2,1,0:T(2,128)(2,1)S(1)}, bf16[32,1,2048]{2,1,0:T(2,128)(2,1)S(1)}, u32[]{:S(2)}, u32[]{:S(2)}) collective-permute-start(bf16[32,1,2048]{2,1,0:T(2,128)(2,1)S(1)} %get-tuple-element.6), channel_id=1, source_target_pairs={{0,6},{1,7},{2,4},{3,5},{4,2},{5,3},{6,0},{7,1},{8,14},{9,15},{10,... | collective-permute-start | bytes 393224 | tf_op jit(solution)/shard_map/ppermute | solution.py:36
  35.5 100.9 %collective-permute-start.4 = (bf16[32,1,2048]{2,1,0:T(2,128)(2,1)S(1)}, bf16[32,1,2048]{2,1,0:T(2,128)(2,1)S(1)}, u32[]{:S(2)}, u32[]{:S(2)}) collective-permute-start(bf16[32,1,2048]{2,1,0:T(2,128)(2,1)S(1)} %get-tuple-element.7), channel_id=1, source_target_pairs={{0,5},{1,4},{2,7},{3,6},{4,1},{5,0},{6,3},{7,2},{8,13},{9,12},{10,... | collective-permute-start | bytes 393224 | tf_op jit(solution)/shard_map/ppermute | solution.py:36
  35.9 100.3 %collective-permute-start.3 = (bf16[32,1,2048]{2,1,0:T(2,128)(2,1)S(1)}, bf16[32,1,2048]{2,1,0:T(2,128)(2,1)S(1)}, u32[]{:S(2)}, u32[]{:S(2)}) collective-permute-start(bf16[32,1,2048]{2,1,0:T(2,128)(2,1)S(1)} %get-tuple-element.8), channel_id=1, source_target_pairs={{0,4},{1,5},{2,6},{3,7},{4,0},{5,1},{6,2},{7,3},{8,12},{9,13},{10,... | collective-permute-start | bytes 393224 | tf_op jit(solution)/shard_map/ppermute | solution.py:36
  38.1 1.9 collective-permute-start
  39.9 45.5 %collective-permute-start.1 = (bf16[32,1,2048]{2,1,0:T(2,128)(2,1)}, bf16[32,1,2048]{2,1,0:T(2,128)(2,1)S(1)}, u32[]{:S(2)}, u32[]{:S(2)}) collective-permute-start(bf16[32,1,2048]{2,1,0:T(2,128)(2,1)} %get-tuple-element.10), channel_id=1, source_target_pairs={{0,2},{1,3},{2,0},{3,1},{4,6},{5,7},{6,4},{7,5},{8,10},{9,11},{10,... | collective-permute-start | bytes 393224 | tf_op jit(solution)/shard_map/ppermute | solution.py:36
  85.4 32.6 %collective-permute-start.2 = (bf16[32,1,2048]{2,1,0:T(2,128)(2,1)}, bf16[32,1,2048]{2,1,0:T(2,128)(2,1)S(1)}, u32[]{:S(2)}, u32[]{:S(2)}) collective-permute-start(bf16[32,1,2048]{2,1,0:T(2,128)(2,1)} %get-tuple-element.9), channel_id=1, source_target_pairs={{0,3},{1,2},{2,1},{3,0},{4,7},{5,6},{6,5},{7,4},{8,11},{9,10},{10,... | collective-permute-start | bytes 393224 | tf_op jit(solution)/shard_map/ppermute | solution.py:36
  136.6 1.0 copy-start
  150.0 52.2 %dynamic-slice-start = ((f32[16384]{0:T(1024)}, s32[]{:T(128)}), f32[4096]{0:T(1024)S(1)}, s32[]{:S(2)}) async-start(f32[16384]{0:T(1024)} %param.5, s32[]{:T(128)} %select_n.71), calls=%async_computation.3 | async-start | bytes 33280 | tf_op jit(solution)/shard_map/dynamic_slice | solution.py:50
Sparse Core Ops, SparseCore 0:
  28.1 121.8 all-gather.2
  151.9 50.2 all-gather.4
